TPU v7x, 32 devices: a whole 2x2x4 slice. The times are simulated.
32 devices in a mesh: dp: 8 (over z, x), mp: 4 (over y, core).
Axes of the slice: x: 2, y: 2, z: 4, core: 2. Of those that a mesh axis runs over, the one named last changes fastest.
Arguments:
- rows: float32 [16384, 1280], P(('dp', 'mp')), may hold values from -6 to 6
- lengths: int32 [256], P('dp'), may hold values from 1 to 64, as said below
- freq_class: int32 [256], P(('dp', 'mp')), may hold values from 0 to 2
- freq_table: float32 [3, 1280], replicated, may hold values from -3 to 3
- gain_attn: float32 [1280], replicated, may hold values from 0.5 to 1.5
- gain_mlp: float32 [1280], replicated, may hold values from 0.5 to 1.5
- w_qkv: float32 [3, 1280, 1280], P(None, None, 'mp'), may hold values from -0.15625 to 0.15625
- w_out: float32 [1280, 1280], P('mp'), may hold values from -0.5 to 0.5
- w_gate_up: float32 [2, 1280, 5120], P(None, None, 'mp'), may hold values from -0.15625 to 0.15625
- w_down: float32 [5120, 1280], P('mp'), may hold values from -0.15625 to 0.15625
- cotangent: float32 [16384, 1280], P(('dp', 'mp')), may hold values from -6 to 6
Outputs:
- output: float32 [16384, 1280], P(('dp', 'mp'))
- grad_rows: float32 [16384, 1280], P(('dp', 'mp'))
- grad_qkv: float32 [3, 1280, 1280], P(None, None, 'mp')
- grad_out: float32 [1280, 1280], P('mp')
- grad_gate_up: float32 [2, 1280, 5120], P(None, None, 'mp')
- grad_down: float32 [5120, 1280], P('mp')
- grad_gain_attn: float32 [1280], replicated
- grad_gain_mlp: float32 [1280], replicated
- grad_table: float32 [3, 1280], replicated
Inputs may be any that keep to these rules, and one draw needn't show every extreme that they name: `lengths`: the valid patches of a series are the last of its 64 slots; some series has all 64, and some only one.
All inputs are finite; a program needn't handle non-finite values.
Results may differ from a plain program's by a relative error of at most 0.02.
Values may be sent and summed in bfloat16 or wider, within the bound.
A program may use at most 256 MiB of HBM per device.

v0:
```python
import jax
import jax.numpy as jnp
from jax import lax
from jax.sharding import PartitionSpec as P

HS = 80
NFREQ = 3
SEQ = 64
EPSILON = 1e-06
NEGATIVE = -1e30
HIGHEST = lax.Precision.HIGHEST


def rotate(values, cosines, sines):
    half_width = values.shape[-1] // 2
    first_half = values[..., :half_width]
    second_half = values[..., half_width:]
    return jnp.concatenate(
        [first_half * cosines - second_half * sines, second_half * cosines + first_half * sines], -1
    )


def series_tables(series_lengths):
    places = jnp.arange(SEQ, dtype=jnp.int32)
    starts = SEQ - series_lengths
    valid_mask = places[None, :] >= starts[:, None]
    positions = (places[None, :] - starts[:, None]).astype(jnp.float32)
    frequency = 10000.0 ** (-2.0 * jnp.arange(HS // 2, dtype=jnp.float32) / HS)
    angles = positions[:, :, None] * frequency[None, None, :]
    return (valid_mask, jnp.cos(angles)[:, :, None, :], jnp.sin(angles)[:, :, None, :])


def allowed_pairs(valid_mask):
    places = jnp.arange(SEQ, dtype=jnp.int32)
    causal = places[:, None] >= places[None, :]
    itself = places[:, None] == places[None, :]
    return causal[None, None] & (valid_mask[:, None, None, :] | itself[None, None])


def norm_forward(values, gain):
    inverse = lax.rsqrt(jnp.mean(values * values, -1, keepdims=True) + EPSILON)
    return ((values * inverse * gain).astype(jnp.bfloat16), inverse)


def norm_backward(values, inverse, gain, grad_normed):
    normal = values * inverse
    grad_gain = jnp.sum(grad_normed * normal, 0)
    scaled = grad_normed * gain
    grad_values = inverse * (scaled - normal * jnp.mean(scaled * normal, -1, keepdims=True))
    return (grad_values, grad_gain)


def attention_scores(queries, keys, allowed):
    raw_scores = jnp.einsum("sihe,sjhe->shij", queries, keys, preferred_element_type=jnp.float32)
    return jnp.where(allowed, raw_scores * HS ** (-0.5), NEGATIVE)


def body(
    rows,
    lengths,
    freq_class,
    freq_table,
    gain_attn,
    gain_mlp,
    w_qkv,
    w_out,
    w_gate_up,
    w_down,
    cotangent,
):
    local_rows = rows.shape[0]
    mp_index = lax.axis_index("mp")
    series_count = lengths.shape[0]
    group_rows = series_count * SEQ
    heads_width = w_out.shape[0]
    head_count = heads_width // HS
    valid_mask, cosines, sines = series_tables(lengths)
    allowed = allowed_pairs(valid_mask)
    flat_valid = valid_mask.reshape(group_rows).astype(jnp.float32)
    mine_valid = lax.dynamic_slice_in_dim(flat_valid, mp_index * local_rows, local_rows)[:, None]
    classes = jnp.repeat(freq_class, SEQ)
    onehot = (classes[:, None] == jnp.arange(NFREQ, dtype=jnp.int32)[None, :]).astype(jnp.float32)
    start_rows = rows + jnp.dot(onehot, freq_table, precision=HIGHEST)
    normed_mine, inverse_attn = norm_forward(start_rows, gain_attn)
    normed = lax.all_gather(normed_mine, "mp", axis=0, tiled=True)
    qkv_low = w_qkv.astype(jnp.bfloat16)
    projected = jnp.einsum("td,cdf->ctf", normed, qkv_low, preferred_element_type=jnp.float32)
    projected = projected.reshape(3, series_count, SEQ, head_count, HS)
    queries = rotate(projected[0], cosines, sines).astype(jnp.bfloat16)
    keys = rotate(projected[1], cosines, sines).astype(jnp.bfloat16)
    values = projected[2].astype(jnp.bfloat16)
    scores = attention_scores(queries, keys, allowed)
    row_max = jnp.max(scores, -1, keepdims=True)
    exponent = jnp.exp(scores - row_max)
    row_total = jnp.sum(exponent, -1, keepdims=True)
    log_total = row_max + jnp.log(row_total)
    attention = (exponent / row_total).astype(jnp.bfloat16)
    mixed = jnp.einsum("shij,sjhe->sihe", attention, values, preferred_element_type=jnp.float32)
    mixed = mixed.reshape(group_rows, heads_width).astype(jnp.bfloat16)
    out_low = w_out.astype(jnp.bfloat16)
    attn_part = jnp.dot(mixed, out_low, preferred_element_type=jnp.float32)
    after_attn = start_rows + lax.psum_scatter(
        attn_part.astype(jnp.bfloat16), "mp", scatter_dimension=0, tiled=True
    ).astype(jnp.float32)
    normed_mlp_mine, inverse_mlp = norm_forward(after_attn, gain_mlp)
    normed_mlp = lax.all_gather(normed_mlp_mine, "mp", axis=0, tiled=True)
    gate_up_low = w_gate_up.astype(jnp.bfloat16)
    gate_up = jnp.einsum("td,cdf->ctf", normed_mlp, gate_up_low, preferred_element_type=jnp.float32)
    gate_pre = gate_up[0]
    up_pre = gate_up[1]
    sigmoid_gate = jax.nn.sigmoid(gate_pre)
    activated = gate_pre * sigmoid_gate
    hidden = (activated * up_pre).astype(jnp.bfloat16)
    down_low = w_down.astype(jnp.bfloat16)
    mlp_part = jnp.dot(hidden, down_low, preferred_element_type=jnp.float32)
    output = after_attn + lax.psum_scatter(
        mlp_part.astype(jnp.bfloat16), "mp", scatter_dimension=0, tiled=True
    ).astype(jnp.float32)
    grad_output = cotangent * mine_valid
    grad_down_in = lax.all_gather(grad_output.astype(jnp.bfloat16), "mp", axis=0, tiled=True)
    grad_down = jnp.einsum("tf,td->fd", hidden, grad_down_in, preferred_element_type=jnp.float32)
    grad_hidden = jnp.einsum(
        "td,fd->tf", grad_down_in, down_low, preferred_element_type=jnp.float32
    )
    grad_gate = grad_hidden * up_pre * (sigmoid_gate * (1.0 + gate_pre * (1.0 - sigmoid_gate)))
    grad_up = grad_hidden * activated
    grad_pre = jnp.stack([grad_gate, grad_up]).astype(jnp.bfloat16)
    grad_gate_up = jnp.einsum(
        "td,ctf->cdf", normed_mlp, grad_pre, preferred_element_type=jnp.float32
    )
    mlp_back_part = jnp.einsum(
        "ctf,cdf->td", grad_pre, gate_up_low, preferred_element_type=jnp.float32
    )
    grad_normed_mlp = lax.psum_scatter(
        mlp_back_part.astype(jnp.bfloat16), "mp", scatter_dimension=0, tiled=True
    ).astype(jnp.float32)
    grad_rows_mlp, grad_gain_mlp = norm_backward(after_attn, inverse_mlp, gain_mlp, grad_normed_mlp)
    grad_after = grad_output + grad_rows_mlp
    grad_attn_in = lax.all_gather(grad_after.astype(jnp.bfloat16), "mp", axis=0, tiled=True)
    grad_out = jnp.einsum("tf,td->fd", mixed, grad_attn_in, preferred_element_type=jnp.float32)
    grad_mixed = jnp.einsum("td,fd->tf", grad_attn_in, out_low, preferred_element_type=jnp.float32)
    grad_mixed = grad_mixed.astype(jnp.bfloat16).reshape(series_count, SEQ, head_count, HS)
    attention_again = jnp.exp(attention_scores(queries, keys, allowed) - log_total)
    grad_attention = jnp.einsum(
        "sihe,sjhe->shij", grad_mixed, values, preferred_element_type=jnp.float32
    )
    grad_values = jnp.einsum(
        "shij,sihe->sjhe",
        attention_again.astype(jnp.bfloat16),
        grad_mixed,
        preferred_element_type=jnp.float32,
    )
    row_dot = jnp.sum(attention_again * grad_attention, -1, keepdims=True)
    grad_scores = (attention_again * (grad_attention - row_dot)).astype(jnp.bfloat16)
    grad_queries = jnp.einsum(
        "shij,sjhe->sihe", grad_scores, keys, preferred_element_type=jnp.float32
    ) * HS ** (-0.5)
    grad_keys = jnp.einsum(
        "shij,sihe->sjhe", grad_scores, queries, preferred_element_type=jnp.float32
    ) * HS ** (-0.5)
    grad_projected = jnp.stack(
        [rotate(grad_queries, cosines, -sines), rotate(grad_keys, cosines, -sines), grad_values]
    )
    grad_projected = grad_projected.reshape(3, group_rows, heads_width).astype(jnp.bfloat16)
    grad_qkv = jnp.einsum("td,ctf->cdf", normed, grad_projected, preferred_element_type=jnp.float32)
    attn_back_part = jnp.einsum(
        "ctf,cdf->td", grad_projected, qkv_low, preferred_element_type=jnp.float32
    )
    grad_normed = lax.psum_scatter(
        attn_back_part.astype(jnp.bfloat16), "mp", scatter_dimension=0, tiled=True
    ).astype(jnp.float32)
    grad_rows_attn, grad_gain_attn = norm_backward(start_rows, inverse_attn, gain_attn, grad_normed)
    grad_rows = grad_after + grad_rows_attn
    grad_table = jnp.dot(onehot.T, grad_rows, precision=HIGHEST)
    grad_gain_attn, grad_gain_mlp, grad_table, token_total = lax.psum(
        (grad_gain_attn, grad_gain_mlp, grad_table, jnp.sum(mine_valid)), ("dp", "mp")
    )
    grad_qkv, grad_out, grad_gate_up, grad_down = (
        lax.psum(grad_qkv.astype(jnp.bfloat16), "dp").astype(jnp.float32),
        lax.psum(grad_out.astype(jnp.bfloat16), "dp").astype(jnp.float32),
        lax.psum(grad_gate_up.astype(jnp.bfloat16), "dp").astype(jnp.float32),
        lax.psum(grad_down.astype(jnp.bfloat16), "dp").astype(jnp.float32),
    )
    root_scale = lax.rsqrt(token_total)
    return (
        output,
        grad_rows,
        grad_qkv * root_scale,
        grad_out * root_scale,
        grad_gate_up * root_scale,
        grad_down * root_scale,
        grad_gain_attn * root_scale,
        grad_gain_mlp * root_scale,
        grad_table * root_scale,
    )


def solution(mesh):
    return jax.shard_map(
        body,
        mesh=mesh,
        in_specs=(
            P(("dp", "mp"), None),
            P("dp"),
            P(("dp", "mp")),
            P(),
            P(),
            P(),
            P(None, None, "mp"),
            P("mp", None),
            P(None, None, "mp"),
            P("mp", None),
            P(("dp", "mp"), None),
        ),
        out_specs=(
            P(("dp", "mp"), None),
            P(("dp", "mp"), None),
            P(None, None, "mp"),
            P("mp", None),
            P(None, None, "mp"),
            P("mp", None),
            P(),
            P(),
            P(),
        ),
        check_vma=False,
    )
```

profile of v0, /device:TPU:0, one launch (start us, length us, event | category | flops | bytes accessed | tf_op | source)
XLA Modules:
  0.0 1067.2 jit_solution(17084121526547978977)
XLA Ops:
  8.1 3.2 multiply_reduce_fusion.2
  11.3 1.7 multiply_convert_fusion.5
  13.6 5.8 fusion.48
  19.4 36.9 %all-gather.5.cloned.1.call-done = bf16[2048,1280]{1,0:T(8,128)(2,1)} async-done(((bf16[512,1280]{1,0:T(8,128)(2,1)}), bf16[2048,1280]{1,0:T(8,128)(2,1)}) %all-gather.5.cloned.1.call-update) | async-done | bytes 5242896 | tf_op jit(solution)/shard_map/all_gather | solution.py:85
  56.3 8.7 fusion.10
  66.2 3.0 fusion.61
  69.2 4.9 reshape.176
  74.1 4.7 copy.39
  78.8 5.3 reshape.177
  84.1 5.5 fusion.62
  89.6 4.9 copy.73
  94.5 4.9 copy.72
  99.3 5.3 reshape.178
  104.7 5.5 fusion.63
  110.1 4.9 copy.75
  115.0 4.9 copy.74
  119.9 7.9 subtract_convert_fusion.3
  127.9 3.2 fusion.64
  132.5 1.8 copy-done.20
  135.5 3.3 copy.41
  138.7 4.3 convert_element_type.131
  143.1 7.1 convolution_convert_fusion.2
  150.3 51.5 %reduce-scatter.5.cloned.1.call-done = bf16[512,1280]{1,0:T(8,128)(2,1)} async-done(((bf16[2048,1280]{1,0:T(8,128)(2,1)}), bf16[512,1280]{1,0:T(8,128)(2,1)}) %reduce-scatter.5.cloned.1.call-update) | async-done | bytes 1310736 | tf_op jit(solution)/shard_map/reduce_scatter | solution.py:102
  201.8 1.8 multiply_reduce_fusion.1
  208.6 38.5 %all-gather.7.cloned.1.call-done = bf16[2048,1280]{1,0:T(8,128)(2,1)} async-done(((bf16[512,1280]{1,0:T(8,128)(2,1)}), bf16[2048,1280]{1,0:T(8,128)(2,1)}) %all-gather.7.cloned.1.call-update) | async-done | bytes 5242896 | tf_op jit(solution)/shard_map/all_gather | solution.py:106
  247.0 22.6 %convolution_bitcast_fusion = f32[2,2048,1280]{2,1,0:T(8,128)} fusion(bf16[2048,1280]{1,0:T(8,128)(2,1)} %all-gather.7.cloned.1.call-done, f32[2,1280,1280]{2,1,0:T(8,128)} %param.19), kind=kOutput, calls=%fused_computation.1 | convolution fusion | flops 13425049600 | bytes 39321600 | tf_op jit(solution)/shard_map/td,cdf->ctf/dot_general | solution.py:108
  269.6 20.0 %all-gather.9.cloned.1.call-done = bf16[2048,1280]{1,0:T(8,128)(2,1)} async-done(((bf16[512,1280]{1,0:T(8,128)(2,1)}), bf16[2048,1280]{1,0:T(8,128)(2,1)}) %all-gather.9.cloned.1.call-update) | async-done | bytes 5242896 | tf_op jit(solution)/shard_map/all_gather | solution.py:120
  289.6 21.7 %fusion.9 = (bf16[1,2048,1280]{2,1,0:T(8,128)(2,1)}, bf16[1,2048,1280]{2,1,0:T(8,128)(2,1)}, bf16[2048,1280]{1,0:T(8,128)(2,1)}) fusion(f32[2,2048,1280]{2,1,0:T(8,128)} %convolution_bitcast_fusion, bf16[2048,1280]{1,0:T(8,128)(2,1)} %all-gather.9.cloned.1.call-done, f32[1280,1280]{1,0:T(8,128)} %param.20), kind=kOutput, calls=%fused_computation.25 | convolution fusion | flops 6751846400 | bytes 48496640 | tf_op jit(solution)/shard_map/td,fd->tf/dot_general | solution.py:122
  311.2 21.7 %bitcast_convert_fusion.1 = bf16[2048,1280]{1,0:T(8,128)(2,1)} fusion(bf16[1,2048,1280]{2,1,0:T(8,128)(2,1)} %get-tuple-element.46, bf16[1,2048,1280]{2,1,0:T(8,128)(2,1)} %get-tuple-element.45, f32[2,1280,1280]{2,1,0:T(8,128)} %param.19), kind=kOutput, calls=%fused_computation.7 | convolution fusion | flops 13432913920 | bytes 28835840 | tf_op jit(solution)/shard_map/ctf,cdf->td/dot_general | solution.py:131
  333.0 12.4 %convolution_convert_fusion.1 = bf16[2048,1280]{1,0:T(8,128)(2,1)} fusion(bf16[2048,1280]{1,0:T(8,128)(2,1)} %get-tuple-element.47, f32[1280,1280]{1,0:T(8,128)} %param.20), kind=kOutput, calls=%fused_computation.14 | convolution fusion | flops 6715146240 | bytes 17039360 | tf_op jit(solution)/shard_map/dot_general | solution.py:115
  345.4 39.1 %reduce-scatter.9.cloned.1.call-done = bf16[512,1280]{1,0:T(8,128)(2,1)} async-done(((bf16[2048,1280]{1,0:T(8,128)(2,1)}), bf16[512,1280]{1,0:T(8,128)(2,1)}) %reduce-scatter.9.cloned.1.call-update) | async-done | bytes 1310736 | tf_op jit(solution)/shard_map/reduce_scatter | solution.py:134
  384.5 2.1 fusion.33
  386.7 51.7 %reduce-scatter.7.cloned.1.call-done = bf16[512,1280]{1,0:T(8,128)(2,1)} async-done(((bf16[2048,1280]{1,0:T(8,128)(2,1)}), bf16[512,1280]{1,0:T(8,128)(2,1)}) %reduce-scatter.7.cloned.1.call-update) | async-done | bytes 1310736 | tf_op jit(solution)/shard_map/reduce_scatter | solution.py:116
  438.4 6.3 fusion.59
  444.8 40.5 %all-gather.11.cloned.1.call-done = bf16[2048,1280]{1,0:T(8,128)(2,1)} async-done(((bf16[512,1280]{1,0:T(8,128)(2,1)}), bf16[2048,1280]{1,0:T(8,128)(2,1)}) %all-gather.11.cloned.1.call-update) | async-done | bytes 5242896 | tf_op jit(solution)/shard_map/all_gather | solution.py:139
  485.3 4.9 convolution_convert_fusion.5
  490.2 4.0 reshape.179
  494.2 3.6 copy.43
  497.8 4.5 convert_bitcast_fusion
  508.1 1.8 multiply_bitcast_fusion.1
  509.9 4.7 subtract_convert_fusion
  514.6 2.5 pad_maximum_fusion.6
  517.1 5.0 copy.59
  522.1 3.1 reshape.174
  525.2 5.0 copy.60
  530.1 2.9 reshape.175
  533.0 4.7 pad_maximum_fusion.5
  537.7 5.0 copy.58
  542.6 2.9 reshape.173
  548.6 1.9 copy-done.28
  550.5 9.9 bitcast_convert_fusion
  560.5 12.3 %convolution_convert_fusion.3 = bf16[1280,1280]{1,0:T(8,128)(2,1)} fusion(bf16[2048,1280]{1,0:T(8,128)(2,1)} %get-tuple-element.47, bf16[2048,1280]{1,0:T(8,128)(2,1)} %all-gather.9.cloned.1.call-done), kind=kOutput, calls=%fused_computation.16 | convolution fusion | flops 6712524800 | bytes 13762560 | tf_op jit(solution)/shard_map/tf,td->fd/dot_general | solution.py:121
  572.8 20.2 %fusion.1 = bf16[2,1280,1280]{1,2,0:T(8,128)(2,1)} fusion(bf16[1,2048,1280]{2,1,0:T(8,128)(2,1)} %get-tuple-element.46, bf16[1,2048,1280]{2,1,0:T(8,128)(2,1)} %get-tuple-element.45, bf16[2048,1280]{1,0:T(8,128)(2,1)} %all-gather.7.cloned.1.call-done), kind=kOutput, calls=%fused_computation.13 | convolution fusion | flops 13430292480 | bytes 22282240 | tf_op jit(solution)/shard_map/td,ctf->cdf/dot_general | solution.py:128
  593.1 2.8 convolution_convert_fusion.4
  595.9 6.5 fusion.20
  602.5 9.5 reduce-scatter.11.cloned.1.call-done
  612.0 2.3 fusion.34
  617.7 44.2 %all-reduce = (f32[]{:T(128)}, f32[1280]{0:T(1024)S(1)}, f32[1280]{0:T(1024)S(1)}, f32[3,1280]{1,0:T(4,128)S(1)}) all-reduce(f32[]{:T(128)} %get-tuple-element.39, f32[1280]{0:T(1024)S(1)} %get-tuple-element.29, f32[1280]{0:T(1024)S(1)} %get-tuple-element.27, f32[3,1280]{1,0:T(4,128)S(1)} %fusion.49), channel_id=1, replica_groups=mesh['dp'=8,'mp'=4] {'dp','mp'}, use_global_device_ids=true, to_apply=%region_13.14 | all-reduce | flops 6401 | bytes 51208 | tf_op jit(solution)/shard_map/psum | solution.py:175
  664.4 365.7 %all-reduce.4.cloned.1.call-done = (bf16[3,1280,320]{1,2,0:T(8,128)(2,1)}, bf16[320,1280]{1,0:T(8,128)(2,1)}, bf16[2,1280,1280]{1,2,0:T(8,128)(2,1)}, bf16[1280,1280]{1,0:T(8,128)(2,1)}) async-done(((bf16[3,1280,320]{1,2,0:T(8,128)(2,1)}, bf16[320,1280]{1,0:T(8,128)(2,1)}, bf16[2,1280,1280]{1,2,0:T(8,128)(2,1)}, bf16[1280,1280]{1,0:T(8,128)(2,1)}), (bf16[3,1280,320]{1,2,0:T(8,128)(2,1)}, ...) | async-done | bytes 13107216 | tf_op jit(solution)/shard_map/psum | solution.py:179
  1030.2 2.6 convert_multiply_fusion.7
  1032.7 2.9 convert_multiply_fusion.2
  1036.0 3.7 convert_multiply_fusion.1
  1040.7 5.8 convert_multiply_fusion
  1046.5 13.9 %copy.54 = f32[2,1280,1280]{2,1,0:T(8,128)} copy(f32[2,1280,1280]{1,2,0:T(8,128)} %convert_multiply_fusion) | data formatting | bytes 26214400
  (138 shorter events, 26.0 us)
Async XLA Ops:
  7.2 0.9 copy-start
  7.2 4.1 copy-start.31
  7.2 49.1 %all-gather.5.cloned.1.call-start = ((), (), s32[]{:S(2)}) async-start(), calls=%async_computation.4 | async-start | bytes 6553600 | tf_op jit(solution)/shard_map/all_gather | solution.py:85
  8.1 4.9 copy-start.35
  11.3 190.5 %copy-start.4 = (f32[512,1280]{1,0:T(8,128)}, f32[512,1280]{1,0:T(8,128)S(1)}, u32[]{:S(2)}) copy-start(f32[512,1280]{1,0:T(8,128)S(1)} %get-tuple-element.73) | copy-start | bytes 7864324
  11.3 1.8 copy-start.37
  11.3 1.8 copy-start.33
  13.0 188.8 %reduce-scatter.5.cloned.1.call-start = ((), (), s32[]{:S(2)}) async-start(), calls=%async_computation.5 | async-start | bytes 6553600 | tf_op jit(solution)/shard_map/reduce_scatter | solution.py:102
  127.9 3.3 copy-start.8
  127.9 3.3 copy-start.10
  127.9 3.3 copy-start.12
  127.9 3.3 copy-start.14
  131.2 4.3 copy-start.2
  131.2 3.1 copy-start.20
  150.2 54.8 %copy-start.30 = (f32[1280]{0:T(1024)S(1)}, f32[1280]{0:T(1024)}, u32[]{:S(2)}) copy-start(f32[1280]{0:T(1024)} %param.16) | copy-start | bytes 15364
  150.2 96.8 %all-gather.7.cloned.1.call-start = ((), (), s32[]{:S(2)}) async-start(), calls=%async_computation.6 | async-start | bytes 6553600 | tf_op jit(solution)/shard_map/all_gather | solution.py:106
  203.6 1.5 copy-start.6
  203.6 3.7 copy-start.18
  206.4 83.1 %all-gather.9.cloned.1.call-start = ((), (), s32[]{:S(2)}) async-start(), calls=%async_computation.8 | async-start | bytes 6553600 | tf_op jit(solution)/shard_map/all_gather | solution.py:120
  208.5 176.0 %reduce-scatter.9.cloned.1.call-start = ((), (), s32[]{:S(2)}) async-start(), calls=%async_computation.9 | async-start | bytes 6553600 | tf_op jit(solution)/shard_map/reduce_scatter | solution.py:134
  333.0 105.4 %reduce-scatter.7.cloned.1.call-start = ((), (), s32[]{:S(2)}) async-start(), calls=%async_computation.7 | async-start | bytes 6553600 | tf_op jit(solution)/shard_map/reduce_scatter | solution.py:116
  345.4 39.1 %copy-start.7 = (f32[512,1280]{1,0:T(8,128)S(1)}, f32[512,1280]{1,0:T(8,128)}, u32[]{:S(2)}) copy-start(f32[512,1280]{1,0:T(8,128)} %copy-done.6) | copy-start | bytes 7864324
  345.4 139.9 %all-gather.11.cloned.1.call-start = ((), (), s32[]{:S(2)}) async-start(), calls=%async_computation.10 | async-start | bytes 6553600 | tf_op jit(solution)/shard_map/all_gather | solution.py:139
  444.7 167.3 %reduce-scatter.11.cloned.1.call-start = ((), (), s32[]{:S(2)}) async-start(), calls=%async_computation.11 | async-start | bytes 6553600 | tf_op jit(solution)/shard_map/reduce_scatter | solution.py:169
  497.8 4.5 copy-start.3
  497.8 4.5 copy-start.21
  503.7 1.6 copy-start.13
  503.7 2.2 copy-start.15
  505.9 1.6 copy-start.9
  505.9 2.2 copy-start.11
  508.1 1.8 copy-start.19
  508.1 1.8 copy-start.24
  545.5 2.9 copy-start.23
  548.5 1.9 copy-start.28
  560.4 469.8 %all-reduce.4.cloned.1.call-start = ((), (), s32[]{:S(2)}) async-start(), calls=%async_computation.12 | async-start | bytes 26214400 | tf_op jit(solution)/shard_map/psum | solution.py:179
  560.4 32.6 %slice-start.4 = ((s8[5242880]{0:T(1024)(128)(4,1)}), s8[4194304]{0:T(1024)(128)(4,1)S(1)}, s32[]{:S(2)}) async-start(s8[5242880]{0:T(1024)(128)(4,1)} %bitcast.110), calls=%async_computation.17 | async-start | bytes 8388608
  560.5 35.5 %slice-start.2 = ((s8[5242880]{0:T(1024)(128)(4,1)}), s8[4194304]{0:T(1024)(128)(4,1)S(1)}, s32[]{:S(2)}) async-start(s8[5242880]{0:T(1024)(128)(4,1)} %bitcast.108), calls=%async_computation.15 | async-start | bytes 8388608
  572.8 20.3 %copy-start.27 = (bf16[2048,320]{1,0:T(8,128)(2,1)S(1)}, bf16[2048,320]{1,0:T(8,128)(2,1)}, u32[]{:S(2)}) copy-start(bf16[2048,320]{1,0:T(8,128)(2,1)} %convert_element_type.131) | copy-start | bytes 3932164
  572.8 20.3 %slice-start.5 = ((s8[5242880]{0:T(1024)(128)(4,1)}), s8[1048576]{0:T(1024)(128)(4,1)S(1)}, s32[]{:S(2)}) async-start(s8[5242880]{0:T(1024)(128)(4,1)} %bitcast.110), calls=%async_computation.18 | async-start | bytes 2097152
  572.8 23.1 %slice-start.3 = ((s8[5242880]{0:T(1024)(128)(4,1)}), s8[1048576]{0:T(1024)(128)(4,1)S(1)}, s32[]{:S(2)}) async-start(s8[5242880]{0:T(1024)(128)(4,1)} %bitcast.108), calls=%async_computation.16 | async-start | bytes 2097152
  593.1 2.8 copy-start.29
  602.5 9.5 copy-start.5
  602.5 9.5 copy-start.32
  602.5 9.5 copy-start.34
  612.0 2.3 copy-start.17
  612.0 2.5 copy-start.22
  614.5 2.2 copy-start.36
  615.1 1.5 copy-start.16
  1030.2 2.6 copy-start.26
  1032.7 3.3 copy-start.25
  1032.7 7.0 slice-start
  1036.0 4.7 slice-start.1
  1046.5 13.9 %copy-start.1 = (f32[3,1280]{1,0:T(4,128)S(1)}, f32[3,1280]{1,0:T(4,128)}, u32[]{:S(2)}) copy-start(f32[3,1280]{1,0:T(4,128)} %param.14) | copy-start | bytes 46084
Sparse Core Ops, SparseCore 0:
  13.1 43.1 all-gather.4
  150.3 51.3 reduce-scatter.4
  206.5 40.4 all-gather.6
  249.1 40.4 all-gather.8
  333.1 51.3 reduce-scatter.8
  386.9 51.3 reduce-scatter.6
  444.8 40.4 all-gather.10
  560.5 51.3 reduce-scatter.10
  617.3 412.7 all-reduce.3
where the time goes:
time: 1080 us; the launch traced here: 1070 us
  waiting for transfers between devices  653 us (60%)
  matrix products  168 us (16%)
  local copies, waits for them, and re-layouts  122 us (11%)
  other arithmetic  63.7 us (6%)
  blocking collectives  44.2 us (4%)
  between operations  15.3 us (1%)
    psum x1, waiting for transfers between devices, body(): lax.psum(grad_qkv.astype(jnp.bfloat16), 'dp').astype(jnp.float32)  366 us
    reduce_scatter x1, waiting for transfers between devices, body(): lax.psum_scatter(mlp_part.astype(jnp.bfloat16), 'mp', scatter_dimension=0...  51.7 us
    reduce_scatter x1, waiting for transfers between devices, body(): lax.psum_scatter(attn_part.astype(jnp.bfloat16), 'mp', scatter_dimension=...  51.5 us
    unnamed x95, local copies, waits for them, and re-layouts  46.5 us
    psum x1, blocking collectives, body(): lax.psum((grad_gain_attn, grad_gain_mlp, grad_table, jnp.sum(mine_valid))...  44.2 us
    all_gather x1, waiting for transfers between devices, body(): lax.all_gather(grad_after.astype(jnp.bfloat16), 'mp', axis=0, tiled=True)  40.5 us
    reduce_scatter x1, waiting for transfers between devices, body(): lax.psum_scatter(mlp_back_part.astype(jnp.bfloat16), 'mp', scatter_dimens...  39.1 us
    all_gather x1, waiting for transfers between devices, body(): normed_mlp = lax.all_gather(normed_mlp_mine, 'mp', axis=0, tiled=True)  38.5 us
  transfers between devices with their start and end apart: 9, of which 9 were waited for; matrix products, arithmetic and copies ran while one was open for 9% of the time, Pallas kernels for 0%

commit v1 on v0

--- a/solution.py
+++ b/solution.py
@@ -9,6 +9,11 @@
 EPSILON = 1e-06
 NEGATIVE = -1e30
 HIGHEST = lax.Precision.HIGHEST
+
+
+def gather_and_add(block, axis):
+    parts = lax.all_gather(block, axis)
+    return jnp.sum(parts, axis=0)
 
 
 def rotate(values, cosines, sines):
@@ -176,7 +181,7 @@
         (grad_gain_attn, grad_gain_mlp, grad_table, jnp.sum(mine_valid)), ("dp", "mp")
     )
     grad_qkv, grad_out, grad_gate_up, grad_down = (
-        lax.psum(grad_qkv.astype(jnp.bfloat16), "dp").astype(jnp.float32),
+        gather_and_add(grad_qkv.astype(jnp.bfloat16), "dp").astype(jnp.float32),
         lax.psum(grad_out.astype(jnp.bfloat16), "dp").astype(jnp.float32),
         lax.psum(grad_gate_up.astype(jnp.bfloat16), "dp").astype(jnp.float32),
         lax.psum(grad_down.astype(jnp.bfloat16), "dp").astype(jnp.float32),

time: 1080 us -> 1360 us (1.26)
  waiting for transfers between devices: 653 us -> 920 us
    all_gather x0 -> x1, waiting for transfers between devices: none -> 349 us  [gather_and_add(): parts = lax.all_gather(block, axis)]
    psum x1, waiting for transfers between devices: 366 us -> 287 us  [body(): lax.psum(grad_out.astype(jnp.bfloat16), 'dp').astype(jnp.float32)]
    unnamed x95 -> x83, local copies, waits for them, and re-layouts: 46.5 us -> 45.3 us
  transfers between devices with their start and end apart: 9 -> 10, of which waited for: 9 -> 10; matrix products, arithmetic and copies ran while one was open for 9% -> 9% of each run, Pallas kernels for 0% -> 0%
where the time goes in v1:
time: 1360 us; the launch traced here: 1350 us
  waiting for transfers between devices  920 us (68%)
  matrix products  172 us (13%)
  local copies, waits for them, and re-layouts  120 us (9%)
  other arithmetic  77.1 us (6%)
  blocking collectives  44.6 us (3%)
  between operations  15.6 us (1%)
    all_gather x1, waiting for transfers between devices, gather_and_add(): parts = lax.all_gather(block, axis)  349 us
    psum x1, waiting for transfers between devices, body(): lax.psum(grad_out.astype(jnp.bfloat16), 'dp').astype(jnp.float32)  287 us
    reduce_scatter x1, waiting for transfers between devices, body(): lax.psum_scatter(mlp_part.astype(jnp.bfloat16), 'mp', scatter_dimension=0...  51.7 us
    reduce_scatter x1, waiting for transfers between devices, body(): lax.psum_scatter(attn_part.astype(jnp.bfloat16), 'mp', scatter_dimension=...  51.5 us
    unnamed x83, local copies, waits for them, and re-layouts  45.3 us
    psum x1, blocking collectives, body(): lax.psum((grad_gain_attn, grad_gain_mlp, grad_table, jnp.sum(mine_valid))...  44.6 us
    all_gather x1, waiting for transfers between devices, body(): lax.all_gather(grad_after.astype(jnp.bfloat16), 'mp', axis=0, tiled=True)  40.5 us
    reduce_scatter x1, waiting for transfers between devices, body(): lax.psum_scatter(mlp_back_part.astype(jnp.bfloat16), 'mp', scatter_dimens...  39.1 us
  transfers between devices with their start and end apart: 10, of which 10 were waited for; matrix products, arithmetic and copies ran while one was open for 9% of the time, Pallas kernels for 0%

profile of v1, /device:TPU:0, one launch (start us, length us, event | category | flops | bytes accessed | tf_op | source)
XLA Modules:
  0.0 1350.0 jit_solution(5364075509722360053)
XLA Ops:
  8.1 3.2 multiply_reduce_fusion.2
  13.6 5.8 fusion.48
  19.4 36.9 %all-gather.7.cloned.1.call-done = bf16[2048,1280]{1,0:T(8,128)(2,1)} async-done(((bf16[512,1280]{1,0:T(8,128)(2,1)}), bf16[2048,1280]{1,0:T(8,128)(2,1)}) %all-gather.7.cloned.1.call-update) | async-done | bytes 5242896 | tf_op jit(solution)/shard_map/all_gather | solution.py:90
  56.2 8.7 fusion.10
  66.2 3.0 fusion.61
  69.2 4.9 reshape.177
  74.1 4.6 copy.62
  78.7 5.3 reshape.178
  84.0 5.5 fusion.62
  89.5 4.9 copy.96
  94.4 4.9 copy.95
  99.2 5.3 reshape.179
  104.6 5.5 fusion.63
  110.0 4.9 copy.98
  115.0 4.9 copy.97
  119.8 8.0 subtract_convert_fusion.3
  127.8 3.2 fusion.64
  132.4 1.8 copy-done.20
  135.4 3.3 copy.64
  138.7 4.3 convert_element_type.133
  143.0 7.1 convolution_convert_fusion.2
  150.2 51.5 %reduce-scatter.5.cloned.1.call-done = bf16[512,1280]{1,0:T(8,128)(2,1)} async-done(((bf16[2048,1280]{1,0:T(8,128)(2,1)}), bf16[512,1280]{1,0:T(8,128)(2,1)}) %reduce-scatter.5.cloned.1.call-update) | async-done | bytes 1310736 | tf_op jit(solution)/shard_map/reduce_scatter | solution.py:107
  201.7 1.8 multiply_reduce_fusion.1
  208.5 38.5 %all-gather.9.cloned.1.call-done = bf16[2048,1280]{1,0:T(8,128)(2,1)} async-done(((bf16[512,1280]{1,0:T(8,128)(2,1)}), bf16[2048,1280]{1,0:T(8,128)(2,1)}) %all-gather.9.cloned.1.call-update) | async-done | bytes 5242896 | tf_op jit(solution)/shard_map/all_gather | solution.py:111
  246.9 22.6 %convolution_bitcast_fusion = f32[2,2048,1280]{2,1,0:T(8,128)} fusion(bf16[2048,1280]{1,0:T(8,128)(2,1)} %all-gather.9.cloned.1.call-done, f32[2,1280,1280]{2,1,0:T(8,128)} %param.19), kind=kOutput, calls=%fused_computation.1 | convolution fusion | flops 13425049600 | bytes 39321600 | tf_op jit(solution)/shard_map/td,cdf->ctf/dot_general | solution.py:113
  269.5 19.9 %all-gather.11.cloned.1.call-done = bf16[2048,1280]{1,0:T(8,128)(2,1)} async-done(((bf16[512,1280]{1,0:T(8,128)(2,1)}), bf16[2048,1280]{1,0:T(8,128)(2,1)}) %all-gather.11.cloned.1.call-update) | async-done | bytes 5242896 | tf_op jit(solution)/shard_map/all_gather | solution.py:125
  289.5 21.7 %fusion.9 = (bf16[1,2048,1280]{2,1,0:T(8,128)(2,1)}, bf16[1,2048,1280]{2,1,0:T(8,128)(2,1)}, bf16[2048,1280]{1,0:T(8,128)(2,1)}) fusion(f32[2,2048,1280]{2,1,0:T(8,128)} %convolution_bitcast_fusion, bf16[2048,1280]{1,0:T(8,128)(2,1)} %all-gather.11.cloned.1.call-done, f32[1280,1280]{1,0:T(8,128)} %param.20), kind=kOutput, calls=%fused_computation.25 | convolution fusion | flops 6751846400 | bytes 48496640 | tf_op jit(solution)/shard_map/td,fd->tf/dot_general | solution.py:127
  311.1 21.7 %bitcast_convert_fusion.1 = bf16[2048,1280]{1,0:T(8,128)(2,1)} fusion(bf16[1,2048,1280]{2,1,0:T(8,128)(2,1)} %get-tuple-element.54, bf16[1,2048,1280]{2,1,0:T(8,128)(2,1)} %get-tuple-element.53, f32[2,1280,1280]{2,1,0:T(8,128)} %param.19), kind=kOutput, calls=%fused_computation.7 | convolution fusion | flops 13432913920 | bytes 28835840 | tf_op jit(solution)/shard_map/ctf,cdf->td/dot_general | solution.py:136
  332.9 12.4 convolution_convert_fusion.1
  345.4 39.1 %reduce-scatter.9.cloned.1.call-done = bf16[512,1280]{1,0:T(8,128)(2,1)} async-done(((bf16[2048,1280]{1,0:T(8,128)(2,1)}), bf16[512,1280]{1,0:T(8,128)(2,1)}) %reduce-scatter.9.cloned.1.call-update) | async-done | bytes 1310736 | tf_op jit(solution)/shard_map/reduce_scatter | solution.py:139
  384.4 2.1 fusion.33
  386.6 51.7 %reduce-scatter.7.cloned.1.call-done = bf16[512,1280]{1,0:T(8,128)(2,1)} async-done(((bf16[2048,1280]{1,0:T(8,128)(2,1)}), bf16[512,1280]{1,0:T(8,128)(2,1)}) %reduce-scatter.7.cloned.1.call-update) | async-done | bytes 1310736 | tf_op jit(solution)/shard_map/reduce_scatter | solution.py:121
  438.2 6.3 fusion.59
  444.6 40.5 %all-gather.13.cloned.1.call-done = bf16[2048,1280]{1,0:T(8,128)(2,1)} async-done(((bf16[512,1280]{1,0:T(8,128)(2,1)}), bf16[2048,1280]{1,0:T(8,128)(2,1)}) %all-gather.13.cloned.1.call-update) | async-done | bytes 5242896 | tf_op jit(solution)/shard_map/all_gather | solution.py:144
  485.1 4.9 convolution_convert_fusion.5
  490.0 3.9 reshape.180
  494.0 3.6 copy.66
  497.6 4.5 convert_bitcast_fusion
  509.8 4.7 subtract_convert_fusion
  514.5 2.5 pad_maximum_fusion.6
  517.0 5.0 copy.82
  522.0 3.1 reshape.175
  525.1 5.0 copy.83
  530.1 2.9 reshape.176
  533.0 4.8 pad_maximum_fusion.5
  537.7 5.0 copy.81
  542.7 2.9 reshape.174
  548.6 1.9 copy-done.27
  550.5 10.0 bitcast_convert_fusion
  560.6 12.4 convolution_convert_fusion.3
  573.0 20.2 %fusion.1 = bf16[2,1280,1280]{1,2,0:T(8,128)(2,1)} fusion(bf16[1,2048,1280]{2,1,0:T(8,128)(2,1)} %get-tuple-element.54, bf16[1,2048,1280]{2,1,0:T(8,128)(2,1)} %get-tuple-element.53, bf16[2048,1280]{1,0:T(8,128)(2,1)} %all-gather.9.cloned.1.call-done), kind=kOutput, calls=%fused_computation.13 | convolution fusion | flops 13430292480 | bytes 22282240 | tf_op jit(solution)/shard_map/td,ctf->cdf/dot_general | solution.py:133
  593.3 2.8 convolution_convert_fusion.4
  596.2 9.9 fusion.20
  606.0 6.0 reduce-scatter.11.cloned.1.call-done
  612.1 2.3 fusion.34
  617.8 44.6 %all-reduce = (f32[]{:T(128)}, f32[1280]{0:T(1024)S(1)}, f32[1280]{0:T(1024)S(1)}, f32[3,1280]{1,0:T(4,128)S(1)}) all-reduce(f32[]{:T(128)} %get-tuple-element.47, f32[1280]{0:T(1024)S(1)} %get-tuple-element.38, f32[1280]{0:T(1024)S(1)} %get-tuple-element.36, f32[3,1280]{1,0:T(4,128)S(1)} %fusion.49), channel_id=1, replica_groups=mesh['dp'=8,'mp'=4] {'dp','mp'}, use_global_device_ids=true, to_apply=%region_13.14 | all-reduce | flops 6401 | bytes 51208 | tf_op jit(solution)/shard_map/psum | solution.py:180
  664.9 286.8 %all-reduce.4.cloned.1.call-done = (bf16[320,1280]{1,0:T(8,128)(2,1)}, bf16[2,1280,1280]{1,2,0:T(8,128)(2,1)}, bf16[1280,1280]{1,0:T(8,128)(2,1)}) async-done(((bf16[320,1280]{1,0:T(8,128)(2,1)}, bf16[2,1280,1280]{1,2,0:T(8,128)(2,1)}, bf16[1280,1280]{1,0:T(8,128)(2,1)}), (bf16[320,1280]{1,0:T(8,128)(2,1)}, bf16[2,1280,1280]{1,2,0:T(8,128)(2,1)}, bf16[1280,1280]{1,0:T(8,128)(2,1)})) %all-reduce.4.cloned.1.call-update) | async-done | bytes 10649616 | tf_op jit(solution)/shard_map/psum | solution.py:185
  951.8 9.1 convert_multiply_fusion
  960.8 14.1 %copy.77 = f32[2,1280,1280]{2,1,0:T(8,128)} copy(f32[2,1280,1280]{1,2,0:T(8,128)} %convert_multiply_fusion) | data formatting | bytes 26214400
  974.9 2.4 convert_multiply_fusion.7
  977.3 3.2 convert_multiply_fusion.1
  980.5 348.8 %all-gather.15.cloned.1.call-done = bf16[24,1280,320]{1,2,0:T(8,128)(2,1)} async-done(((bf16[3,1280,320]{1,2,0:T(8,128)(2,1)}), bf16[24,1280,320]{1,2,0:T(8,128)(2,1)}) %all-gather.15.cloned.1.call-update) | async-done | bytes 19660816 | tf_op jit(solution)/shard_map/all_gather | solution.py:15
  1329.3 10.9 reduce_sum.99
  1340.3 2.7 convert_multiply_fusion.2
  (128 shorter events, 27.9 us)
Async XLA Ops:
  7.2 0.9 copy-start
  7.2 4.1 copy-start.29
  7.2 49.0 %all-gather.7.cloned.1.call-start = ((), (), s32[]{:S(2)}) async-start(), calls=%async_computation.4 | async-start | bytes 6553600 | tf_op jit(solution)/shard_map/all_gather | solution.py:90
  8.1 4.9 copy-start.33
  11.3 190.4 %copy-start.4 = (f32[512,1280]{1,0:T(8,128)}, f32[512,1280]{1,0:T(8,128)S(1)}, u32[]{:S(2)}) copy-start(f32[512,1280]{1,0:T(8,128)S(1)} %get-tuple-element.81) | copy-start | bytes 7864324
  11.3 1.8 copy-start.35
  11.3 1.7 copy-start.31
  12.9 188.8 %reduce-scatter.5.cloned.1.call-start = ((), (), s32[]{:S(2)}) async-start(), calls=%async_computation.5 | async-start | bytes 6553600 | tf_op jit(solution)/shard_map/reduce_scatter | solution.py:107
  127.8 3.3 copy-start.8
  127.8 3.3 copy-start.10
  127.8 3.3 copy-start.12
  127.8 3.3 copy-start.14
  131.1 4.3 copy-start.2
  131.1 3.1 copy-start.20
  150.2 54.8 %copy-start.28 = (f32[1280]{0:T(1024)S(1)}, f32[1280]{0:T(1024)}, u32[]{:S(2)}) copy-start(f32[1280]{0:T(1024)} %param.16) | copy-start | bytes 15364
  150.2 96.8 %all-gather.9.cloned.1.call-start = ((), (), s32[]{:S(2)}) async-start(), calls=%async_computation.6 | async-start | bytes 6553600 | tf_op jit(solution)/shard_map/all_gather | solution.py:111
  203.5 1.5 copy-start.6
  203.5 3.7 copy-start.18
  206.3 83.1 %all-gather.11.cloned.1.call-start = ((), (), s32[]{:S(2)}) async-start(), calls=%async_computation.8 | async-start | bytes 6553600 | tf_op jit(solution)/shard_map/all_gather | solution.py:125
  208.4 176.0 %reduce-scatter.9.cloned.1.call-start = ((), (), s32[]{:S(2)}) async-start(), calls=%async_computation.9 | async-start | bytes 6553600 | tf_op jit(solution)/shard_map/reduce_scatter | solution.py:139
  332.9 105.4 %reduce-scatter.7.cloned.1.call-start = ((), (), s32[]{:S(2)}) async-start(), calls=%async_computation.7 | async-start | bytes 6553600 | tf_op jit(solution)/shard_map/reduce_scatter | solution.py:121
  345.3 39.1 %copy-start.7 = (f32[512,1280]{1,0:T(8,128)S(1)}, f32[512,1280]{1,0:T(8,128)}, u32[]{:S(2)}) copy-start(f32[512,1280]{1,0:T(8,128)} %copy-done.6) | copy-start | bytes 7864324
  345.3 139.8 %all-gather.13.cloned.1.call-start = ((), (), s32[]{:S(2)}) async-start(), calls=%async_computation.10 | async-start | bytes 6553600 | tf_op jit(solution)/shard_map/all_gather | solution.py:144
  444.5 167.5 %reduce-scatter.11.cloned.1.call-start = ((), (), s32[]{:S(2)}) async-start(), calls=%async_computation.11 | async-start | bytes 6553600 | tf_op jit(solution)/shard_map/reduce_scatter | solution.py:174
  497.6 4.6 copy-start.3
  497.6 4.5 copy-start.21
  503.5 1.6 copy-start.13
  503.6 2.2 copy-start.15
  505.8 1.6 copy-start.9
  505.8 2.2 copy-start.11
  508.0 1.8 copy-start.19
  508.0 1.8 copy-start.24
  545.6 2.9 copy-start.23
  548.6 1.9 copy-start.27
  560.5 391.2 %all-reduce.4.cloned.1.call-start = ((), (), s32[]{:S(2)}) async-start(), calls=%async_computation.13 | async-start | bytes 21299200 | tf_op jit(solution)/shard_map/psum | solution.py:185
  560.6 32.7 %slice-start = ((s8[5242880]{0:T(1024)(128)(4,1)}), s8[4194304]{0:T(1024)(128)(4,1)S(1)}, s32[]{:S(2)}) async-start(s8[5242880]{0:T(1024)(128)(4,1)} %bitcast.108), calls=%async_computation.14 | async-start | bytes 8388608
  573.0 20.3 %copy-start.26 = (bf16[2048,320]{1,0:T(8,128)(2,1)S(1)}, bf16[2048,320]{1,0:T(8,128)(2,1)}, u32[]{:S(2)}) copy-start(bf16[2048,320]{1,0:T(8,128)(2,1)} %convert_element_type.133) | copy-start | bytes 3932164
  573.0 20.3 %slice-start.1 = ((s8[5242880]{0:T(1024)(128)(4,1)}), s8[1048576]{0:T(1024)(128)(4,1)S(1)}, s32[]{:S(2)}) async-start(s8[5242880]{0:T(1024)(128)(4,1)} %bitcast.108), calls=%async_computation.15 | async-start | bytes 2097152
  596.1 16.0 %copy-start.30 = (f32[1280]{0:T(1024)S(1)}, f32[1280]{0:T(1024)}, u32[]{:S(2)}) copy-start(f32[1280]{0:T(1024)} %param.15) | copy-start | bytes 15364
  596.1 16.0 %copy-start.32 = (f32[512]{0:T(512)S(1)}, f32[512]{0:T(512)}, u32[]{:S(2)}) copy-start(f32[512]{0:T(512)} %copy-done.31) | copy-start | bytes 6148
  596.1 733.2 %all-gather.15.cloned.1.call-start = ((), (), s32[]{:S(2)}) async-start(), calls=%async_computation.12 | async-start | bytes 22118400 | tf_op jit(solution)/shard_map/all_gather | solution.py:15
  596.2 15.9 %copy-start.5 = (f32[512,1280]{1,0:T(8,128)S(1)}, f32[512,1280]{1,0:T(8,128)}, u32[]{:S(2)}) copy-start(f32[512,1280]{1,0:T(8,128)} %copy-done.4) | copy-start | bytes 7864324
  612.1 2.3 copy-start.17
  612.1 2.5 copy-start.22
  614.6 2.2 copy-start.34
  615.3 1.5 copy-start.16
  960.8 16.5 %copy-start.25 = (bf16[1280,1280]{1,0:T(8,128)(2,1)S(1)}, bf16[1280,1280]{1,0:T(8,128)(2,1)}, u32[]{:S(2)}) copy-start(bf16[1280,1280]{1,0:T(8,128)(2,1)} %get-tuple-element.46) | copy-start | bytes 9830404
  1329.3 13.6 %copy-start.1 = (f32[3,1280]{1,0:T(4,128)S(1)}, f32[3,1280]{1,0:T(4,128)}, u32[]{:S(2)}) copy-start(f32[3,1280]{1,0:T(4,128)} %param.14) | copy-start | bytes 46084
Sparse Core Ops, SparseCore 0:
  13.1 43.1 all-gather.6
  150.3 51.3 reduce-scatter.4
  206.5 40.4 all-gather.8
  249.0 40.4 all-gather.10
  333.0 51.3 reduce-scatter.8
  386.8 51.3 reduce-scatter.6
  444.7 40.4 all-gather.12
  560.6 51.3 reduce-scatter.10
  617.1 334.5 all-reduce.3
  953.1 376.1 all-gather.14
